TPU v7x, 32 devices: a whole 2x2x4 slice. The times are simulated.
32 devices in a mesh: expert: 16 (over z, y, x), seq: 2 (over core).
Axes of the slice: x: 2, y: 2, z: 4, core: 2. Of those that a mesh axis runs over, the one named last changes fastest.
Arguments:
- out_grad: bfloat16 [4096, 7168], P(('expert', 'seq')), may hold values from -6 to 6
- route_ids: int32 [4096, 8], P('expert'), may hold values from 0 to 255, all different within a row
- route_weights: float32 [4096, 8], P('expert'), may hold values from 0.2 to 1
- gate_pre: bfloat16 [16, 192, 1024], P('expert', None, 'seq'), may hold values from -5 to 5
- up_pre: bfloat16 [16, 192, 1024], P('expert', None, 'seq'), may hold values from -5 to 5
- w_gate: bfloat16 [16, 7168, 1024], P('expert', None, 'seq'), may hold values from -0.75 to 0.75
- w_up: bfloat16 [16, 7168, 1024], P('expert', None, 'seq'), may hold values from -0.75 to 0.75
- w_down: bfloat16 [16, 1024, 7168], P('expert', 'seq'), may hold values from -0.0078125 to 0.0078125
Outputs:
- in_grad: bfloat16 [4096, 7168], P(('expert', 'seq'))
- weight_grad: bfloat16 [4096, 8], P(('expert', 'seq'))
Inputs may be any that keep to these rules, and one draw needn't show every extreme that they name: `route_ids`: each row names 8 different experts; only experts below 16 are held in this window, the others are left to other windows.
All inputs are finite; a program needn't handle non-finite values.
Results may differ from a plain program's by a relative error of at most 0.0065.
Values may be sent and summed in bfloat16 or wider, within the bound.
A program may use at most 192 MiB of HBM per device.

v0:
```python
import jax
import jax.numpy as jnp
from jax import lax
from jax.sharding import PartitionSpec as P

BF = jnp.bfloat16
F32 = jnp.float32
NT = (((1,), (1,)), ((), ()))
NN = (((1,), (0,)), ((), ()))
TN = (((0,), (0,)), ((), ()))


def silu_parts(value):
    sigma = jax.nn.sigmoid(value)
    return (value * sigma, sigma * (1.0 + value * (1.0 - sigma)))


def dot(a, b, dims):
    return lax.dot_general(a, b, dims, preferred_element_type=F32)


def swap(value):
    return lax.ppermute(value, "seq", [(0, 1), (1, 0)])


def ordered(mine, theirs, seq_at, axis):
    low = jnp.where(seq_at == 0, mine, theirs)
    high = jnp.where(seq_at == 0, theirs, mine)
    return jnp.concatenate([low, high], axis=axis)


def routing(ids, weights, experts, capacity):
    tokens = ids.shape[0]
    same = ids[:, :, None] == jnp.arange(experts, dtype=jnp.int32)
    hit = jnp.any(same, axis=1)
    weight = jnp.sum(jnp.where(same, weights[:, :, None], 0.0), axis=1)
    row = jnp.arange(tokens, dtype=jnp.int32)
    earlier = (row[None, :] < row[:, None]).astype(BF)
    position = dot(earlier, hit.astype(BF), NN)
    slot = jnp.where(hit, position, float(capacity))
    return slot, weight


def on_device_xla(out_grad, route_ids, route_weights, gate_pre, up_pre, w_gate, w_up, w_down):
    n_expert = lax.axis_size("expert")
    seq_at = lax.axis_index("seq")
    own, width = out_grad.shape
    half = width // 2
    experts = n_expert
    slots = gate_pre.shape[1]
    capacity = slots // n_expert
    slot, weight = routing(route_ids, route_weights, experts, capacity)
    table = (slot[:, :, None] == jnp.arange(capacity, dtype=F32)).reshape(2 * own, slots)
    w_all = jnp.broadcast_to(weight[:, :, None], (2 * own, experts, capacity)).reshape(2 * own, slots)
    w_all = jnp.where(table, w_all, 0.0)
    w_hi = w_all.astype(BF)
    w_lo = (w_all - w_hi.astype(F32)).astype(BF)
    mine = lax.dynamic_slice_in_dim(out_grad, seq_at * half, half, 1)
    other = lax.dynamic_slice_in_dim(out_grad, (1 - seq_at) * half, half, 1)
    tokens = ordered(mine, swap(other), seq_at, 0)
    outgoing = dot(table.astype(BF), tokens, TN).astype(BF).reshape(experts, capacity, half)
    received = lax.all_to_all(outgoing, "expert", split_axis=0, concat_axis=0, tiled=True)
    received = received.reshape(slots, half)
    slot_grad = ordered(received, swap(received), seq_at, 1)
    hidden_grad = dot(slot_grad, w_down[0], NT)
    active, slope = silu_parts(gate_pre[0].astype(F32))
    up_part = up_pre[0].astype(F32)
    score = jnp.sum(hidden_grad * active * up_part, axis=1).astype(BF)
    gate_diff = (hidden_grad * up_part * slope).astype(BF)
    up_diff = (hidden_grad * active).astype(BF)
    part = (dot(gate_diff, w_gate[0], NT) + dot(up_diff, w_up[0], NT)).astype(BF)
    score = lax.optimization_barrier(score)
    part = lax.optimization_barrier(part)
    keep = lax.dynamic_slice_in_dim(part, seq_at * half, half, 1)
    give = lax.dynamic_slice_in_dim(part, (1 - seq_at) * half, half, 1)
    total = (keep.astype(F32) + swap(give).astype(F32)).astype(BF)
    total_score = (score.astype(F32) + swap(score).astype(F32)).astype(BF)
    back = lax.all_to_all(
        total.reshape(n_expert, capacity, half), "expert", split_axis=0, concat_axis=0, tiled=True
    ).reshape(slots, half)
    back_score = lax.all_to_all(
        total_score.reshape(n_expert, capacity), "expert", split_axis=0, concat_axis=0, tiled=True
    ).reshape(slots)
    rows = (dot(w_hi, back, NN) + dot(w_lo, back, NN)).astype(BF)
    keep = lax.dynamic_slice_in_dim(rows, seq_at * own, own, 0)
    give = lax.dynamic_slice_in_dim(rows, (1 - seq_at) * own, own, 0)
    in_grad = ordered(keep, swap(give), seq_at, 1)
    own_table = lax.dynamic_slice_in_dim(table, seq_at * own, own, 0)
    own_ids = lax.dynamic_slice_in_dim(route_ids, seq_at * own, own, 0)
    of_expert = jnp.sum(
        jnp.where(own_table, back_score.astype(F32)[None, :], 0.0).reshape(own, experts, capacity),
        axis=2,
    )
    same = own_ids[:, :, None] == jnp.arange(experts, dtype=jnp.int32)
    weight_grad = jnp.sum(jnp.where(same, of_expert[:, None, :], 0.0), axis=2)
    return in_grad, weight_grad.astype(BF)


def solution(mesh):
    in_specs = (
        P(("expert", "seq"), None),
        P("expert", None),
        P("expert", None),
        P("expert", None, "seq"),
        P("expert", None, "seq"),
        P("expert", None, "seq"),
        P("expert", None, "seq"),
        P("expert", "seq", None),
    )
    out_specs = (P(("expert", "seq"), None), P(("expert", "seq"), None))
    return jax.shard_map(
        on_device_xla, mesh=mesh, in_specs=in_specs, out_specs=out_specs, check_vma=False
    )
```

profile of v0, /device:TPU:0, one launch (start us, length us, event | category | flops | bytes accessed | tf_op | source)
XLA Modules:
  0.0 150.7 jit_solution(17988192414317269355)
XLA Ops:
  0.7 1.4 constant_dynamic-slice_fusion.3
  2.0 0.6 collective-permute-start
  2.7 0.2 convolution_select_fusion
  3.1 1.7 %collective-permute-done = bf16[128,3584]{1,0:T(8,128)(2,1)} collective-permute-done((bf16[128,3584]{1,0:T(8,128)(2,1)S(1)}, bf16[128,3584]{1,0:T(8,128)(2,1)}, u32[]{:S(2)}, u32[]{:S(2)}) %collective-permute-start) | collective-permute-done | bytes 917536 | tf_op jit(solution)/shard_map/ppermute | solution.py:23
  4.8 1.5 broadcast_select_fusion.5
  6.3 0.5 convolution_convert_fusion
  6.8 0.4 reshape.56
  7.2 52.2 %all_to_all.20 = bf16[16,12,3584]{2,1,0:T(8,128)(2,1)} all-to-all(bf16[16,12,3584]{2,1,0:T(8,128)(2,1)S(1)} %reshape.56), channel_id=1, replica_groups=mesh['expert'=16,'seq'=2] {'expert'}, dimensions={0} | all-to-all | bytes 2752512 | tf_op jit(solution)/shard_map/all_to_all | solution.py:62
  59.4 2.4 %reshape.57 = bf16[192,3584]{1,0:T(8,128)(2,1)S(1)} reshape(bf16[16,12,3584]{2,1,0:T(8,128)(2,1)} %all_to_all.20) | data formatting | bytes 2752512 | tf_op jit(solution)/shard_map/reshape | solution.py:63
  61.9 3.1 %collective-permute-done.1 = bf16[192,3584]{1,0:T(8,128)(2,1)S(1)} collective-permute-done((bf16[192,3584]{1,0:T(8,128)(2,1)S(1)}, bf16[192,3584]{1,0:T(8,128)(2,1)S(1)}, u32[]{:S(2)}, u32[]{:S(2)}) %collective-permute-start.1) | collective-permute-done | bytes 1376288 | tf_op jit(solution)/shard_map/ppermute | solution.py:23
  65.0 0.2 broadcast_select_fusion.1
  65.3 5.9 %fusion.16 = (bf16[192]{0:T(256)(128)(2,1)S(1)}, f32[192,512]{1,0:T(8,128)S(1)}) fusion(bf16[1,192,512]{2,1,0:T(8,128)(2,1)S(1)} %copy-done.3, bf16[1,192,512]{2,1,0:T(8,128)(2,1)S(1)} %copy-done.2, bf16[1,512,7168]{2,1,0:T(8,128)(2,1)} %param.15, bf16[192,3584]{1,0:T(8,128)(2,1)S(1)} %get-tuple-element.5, bf16[192,3584]{1,0:T(8,128)(2,1)S(1)} %get-tuple-element.4), kind=kOutput, calls=%fused_computation.34 | convolution fusion | flops 1415675648 | bytes 10879360 | tf_op jit(solution)/shard_map/dot_general | solution.py:19
  71.2 0.3 slice-done.1
  71.5 2.5 %fusion.2 = f32[192,7168]{1,0:T(8,128)S(1)} fusion(bf16[1,7168,512]{2,1,0:T(8,128)(2,1)S(1)} %bitcast.47, f32[192,512]{1,0:T(8,128)S(1)} %get-tuple-element.9, bf16[1,192,512]{2,1,0:T(8,128)(2,1)S(1)} %copy-done.3, bf16[1,192,512]{2,1,0:T(8,128)(2,1)S(1)} %copy-done.2), kind=kOutput, calls=%fused_computation.3 | convolution fusion | flops 1410465792 | bytes 13631488 | tf_op jit(solution)/shard_map/dot_general | solution.py:19
  74.0 2.6 %fusion = bf16[192,7168]{1,0:T(8,128)(2,1)S(1)} fusion(f32[192,7168]{1,0:T(8,128)S(1)} %fusion.2, bf16[1,7168,512]{2,1,0:T(8,128)(2,1)S(1)} %bitcast.49, f32[192,512]{1,0:T(8,128)S(1)} %get-tuple-element.9, bf16[1,192,512]{2,1,0:T(8,128)(2,1)S(1)} %copy-done.2), kind=kOutput, calls=%fused_computation.1 | convolution fusion | flops 1412726784 | bytes 16187392 | tf_op jit(solution)/shard_map/dot_general | solution.py:19
  76.7 0.2 collective-permute-start.2
  76.9 3.0 %collective-permute-done.2 = bf16[192,3584]{1,0:T(8,128)(2,1)S(1)} collective-permute-done((bf16[192,3584]{1,0:T(8,128)(2,1)S(1)}, bf16[192,3584]{1,0:T(8,128)(2,1)S(1)}, u32[]{:S(2)}, u32[]{:S(2)}) %collective-permute-start.2) | collective-permute-done | bytes 1376288 | tf_op jit(solution)/shard_map/ppermute | solution.py:23
  79.9 0.3 add_convert_fusion
  80.3 1.4 reshape.58
  81.7 3.8 %all-to-all-start.1 = ((bf16[16,12,3584]{2,1,0:T(8,128)(2,1)}), bf16[16,12,3584]{2,1,0:T(8,128)(2,1)S(1)}, u32[]{:S(2)}, u32[]{:S(2)}) async-start(bf16[16,12,3584]{2,1,0:T(8,128)(2,1)} %reshape.58), calls=%async_computation.1 | async-start | bytes 3670016 | tf_op jit(solution)/shard_map/all_to_all | solution.py:78
  85.6 38.8 %all-to-all-done.1 = bf16[16,12,3584]{2,1,0:T(8,128)(2,1)S(1)} async-done(((bf16[16,12,3584]{2,1,0:T(8,128)(2,1)}), bf16[16,12,3584]{2,1,0:T(8,128)(2,1)S(1)}, u32[]{:S(2)}, u32[]{:S(2)}) %all-to-all-start.1) | async-done | bytes 1376288 | tf_op jit(solution)/shard_map/all_to_all | solution.py:78
  124.3 0.7 convolution_bitcast_fusion
  125.0 0.7 fusion.7
  125.7 1.2 copy-done.1
  127.0 0.5 collective-permute-start.4
  127.5 2.0 %collective-permute-done.4 = bf16[192]{0:T(256)(128)(2,1)S(1)} collective-permute-done((bf16[192]{0:T(256)(128)(2,1)S(1)}, bf16[192]{0:T(256)(128)(2,1)S(1)}, u32[]{:S(2)}, u32[]{:S(2)}) %collective-permute-start.4) | collective-permute-done | bytes 416 | tf_op jit(solution)/shard_map/ppermute | solution.py:23
  129.5 0.7 all_to_all.16
  130.2 9.4 %all-to-all-start.2 = ((bf16[16,1,12]{2,1,0:T(2,128)(2,1)}), bf16[16,1,12]{2,1,0:T(2,128)(2,1)S(1)}, u32[]{:S(2)}, u32[]{:S(2)}) async-start(bf16[16,1,12]{2,1,0:T(2,128)(2,1)} %all_to_all.16), calls=%async_computation.2 | async-start | bytes 16384 | tf_op jit(solution)/shard_map/all_to_all | solution.py:81
  139.7 7.3 %all-to-all-done.2 = bf16[16,1,12]{2,1,0:T(2,128)(2,1)S(1)} async-done(((bf16[16,1,12]{2,1,0:T(2,128)(2,1)}), bf16[16,1,12]{2,1,0:T(2,128)(2,1)S(1)}, u32[]{:S(2)}, u32[]{:S(2)}) %all-to-all-start.2) | async-done | bytes 416 | tf_op jit(solution)/shard_map/all_to_all | solution.py:81
  147.2 0.6 select_reduce_fusion.1
  147.8 1.5 broadcast_select_fusion.3
  149.3 1.4 pad_maximum_fusion
  (39 shorter events, 0.9 us)
Async XLA Ops:
  0.6 4.2 %copy-start = (bf16[128,7168]{1,0:T(8,128)(2,1)S(1)}, bf16[128,7168]{1,0:T(8,128)(2,1)}, u32[]{:S(2)}) copy-start(bf16[128,7168]{1,0:T(8,128)(2,1)} %param.8) | copy-start | bytes 5505028
  0.6 2.0 %copy-start.4 = (s32[256,8]{0,1:T(8,128)S(1)}, s32[256,8]{0,1:T(8,128)}, u32[]{:S(2)}) copy-start(s32[256,8]{0,1:T(8,128)} %param.9) | copy-start | bytes 24580
  2.0 2.8 %collective-permute-start = (bf16[128,3584]{1,0:T(8,128)(2,1)S(1)}, bf16[128,3584]{1,0:T(8,128)(2,1)}, u32[]{:S(2)}, u32[]{:S(2)}) collective-permute-start(bf16[128,3584]{1,0:T(8,128)(2,1)S(1)} %constant_dynamic-slice_fusion.3), channel_id=1, source_target_pairs={{0,1},{1,0},{2,3},{3,2},{4,5},{5,4},{6,7},{7,6},{8,9},{9,8},{10,11... | collective-permute-start | bytes 2752520 | tf_op jit(solution)/shard_map/ppermute | solution.py:23
  61.8 3.4 %copy-start.2 = (bf16[1,192,512]{2,1,0:T(8,128)(2,1)S(1)}, bf16[1,192,512]{2,1,0:T(8,128)(2,1)}, u32[]{:S(2)}) copy-start(bf16[1,192,512]{2,1,0:T(8,128)(2,1)} %param.11) | copy-start | bytes 589828
  61.8 3.4 %copy-start.3 = (bf16[1,192,512]{2,1,0:T(8,128)(2,1)S(1)}, bf16[1,192,512]{2,1,0:T(8,128)(2,1)}, u32[]{:S(2)}) copy-start(bf16[1,192,512]{2,1,0:T(8,128)(2,1)} %param.12) | copy-start | bytes 589828
  61.8 3.2 %collective-permute-start.1 = (bf16[192,3584]{1,0:T(8,128)(2,1)S(1)}, bf16[192,3584]{1,0:T(8,128)(2,1)S(1)}, u32[]{:S(2)}, u32[]{:S(2)}) collective-permute-start(bf16[192,3584]{1,0:T(8,128)(2,1)S(1)} %reshape.57), channel_id=1, source_target_pairs={{0,1},{1,0},{2,3},{3,2},{4,5},{5,4},{6,7},{7,6},{8,9},{9,8},{10,11... | collective-permute-start | bytes 4128776 | tf_op jit(solution)/shard_map/ppermute | solution.py:23
  65.0 6.2 %slice-start = ((s8[7340032]{0:T(1024)(128)(4,1)}), s8[4194304]{0:T(1024)(128)(4,1)S(1)}, s32[]{:S(2)}) async-start(s8[7340032]{0:T(1024)(128)(4,1)} %bitcast.46), calls=%async_computation.3 | async-start | bytes 8388608
  65.0 9.0 %slice-start.2 = ((s8[7340032]{0:T(1024)(128)(4,1)}), s8[4194304]{0:T(1024)(128)(4,1)S(1)}, s32[]{:S(2)}) async-start(s8[7340032]{0:T(1024)(128)(4,1)} %bitcast.48), calls=%async_computation.5 | async-start | bytes 8388608
  65.2 6.3 %slice-start.1 = ((s8[7340032]{0:T(1024)(128)(4,1)}), s8[3145728]{0:T(1024)(128)(4,1)S(1)}, s32[]{:S(2)}) async-start(s8[7340032]{0:T(1024)(128)(4,1)} %bitcast.46), calls=%async_computation.4 | async-start | bytes 6291456
  65.2 8.8 %slice-start.3 = ((s8[7340032]{0:T(1024)(128)(4,1)}), s8[3145728]{0:T(1024)(128)(4,1)S(1)}, s32[]{:S(2)}) async-start(s8[7340032]{0:T(1024)(128)(4,1)} %bitcast.48), calls=%async_computation.6 | async-start | bytes 6291456
  76.7 3.2 %collective-permute-start.2 = (bf16[192,3584]{1,0:T(8,128)(2,1)S(1)}, bf16[192,3584]{1,0:T(8,128)(2,1)S(1)}, u32[]{:S(2)}, u32[]{:S(2)}) collective-permute-start(bf16[192,3584]{1,0:T(8,128)(2,1)S(1)} %constant_dynamic-slice_fusion.2), channel_id=1, source_target_pairs={{0,1},{1,0},{2,3},{3,2},{4,5},{5,4},{6,7},{7,6},{8,9},{9,8},{10,11... | collective-permute-start | bytes 4128776 | tf_op jit(solution)/shard_map/ppermute | solution.py:23
  81.7 3.9 %copy-start.5 = (f32[256,8]{0,1:T(8,128)S(1)}, f32[256,8]{0,1:T(8,128)}, u32[]{:S(2)}) copy-start(f32[256,8]{0,1:T(8,128)} %param.10) | copy-start | bytes 24580
  81.7 42.7 %all-to-all-start.1 = ((bf16[16,12,3584]{2,1,0:T(8,128)(2,1)}), bf16[16,12,3584]{2,1,0:T(8,128)(2,1)S(1)}, u32[]{:S(2)}, u32[]{:S(2)}) async-start(bf16[16,12,3584]{2,1,0:T(8,128)(2,1)} %reshape.58), calls=%async_computation.1 | async-start | bytes 3670016 | tf_op jit(solution)/shard_map/all_to_all | solution.py:78
  125.7 1.2 copy-start.1
  127.0 20.9 %collective-permute-start.3 = (bf16[128,3584]{1,0:T(8,128)(2,1)S(1)}, bf16[128,3584]{1,0:T(8,128)(2,1)S(1)}, u32[]{:S(2)}, u32[]{:S(2)}) collective-permute-start(bf16[128,3584]{1,0:T(8,128)(2,1)S(1)} %constant_dynamic-slice_fusion.1), channel_id=1, source_target_pairs={{0,1},{1,0},{2,3},{3,2},{4,5},{5,4},{6,7},{7,6},{8,9},{9,8},{10,11... | collective-permute-start | bytes 2752520 | tf_op jit(solution)/shard_map/ppermute | solution.py:23
  127.0 2.5 %collective-permute-start.4 = (bf16[192]{0:T(256)(128)(2,1)S(1)}, bf16[192]{0:T(256)(128)(2,1)S(1)}, u32[]{:S(2)}, u32[]{:S(2)}) collective-permute-start(bf16[192]{0:T(256)(128)(2,1)S(1)} %get-tuple-element.8), channel_id=1, source_target_pairs={{0,1},{1,0},{2,3},{3,2},{4,5},{5,4},{6,7},{7,6},{8,9},{9,8},{10,11... | collective-permute-start | bytes 1160 | tf_op jit(solution)/shard_map/ppermute | solution.py:23
  130.2 16.7 %all-to-all-start.2 = ((bf16[16,1,12]{2,1,0:T(2,128)(2,1)}), bf16[16,1,12]{2,1,0:T(2,128)(2,1)S(1)}, u32[]{:S(2)}, u32[]{:S(2)}) async-start(bf16[16,1,12]{2,1,0:T(2,128)(2,1)} %all_to_all.16), calls=%async_computation.2 | async-start | bytes 16384 | tf_op jit(solution)/shard_map/all_to_all | solution.py:81
where the time goes:
time: 151 us
  waiting for transfers between devices  55.9 us (37%)
  blocking collectives  52.2 us (35%)
  starting transfers between devices  14.7 us (10%)
  matrix products  13 us (9%)
  local copies, waits for them, and re-layouts  8.23 us (5%)
  other arithmetic  5.79 us (4%)
    all_to_all x1, blocking collectives, on_device_xla(): lax.all_to_all(outgoing, 'expert', split_axis=0, concat_axis=0, tiled=True)  52.2 us
    all_to_all x1, waiting for transfers between devices, on_device_xla(): lax.all_to_all(total.reshape(n_expert, capacity, half), 'expert', split_a...  38.8 us
    dot_general x7, matrix products, dot(): return lax.dot_general(a, b, dims, preferred_element_type=F32)  13 us
    ppermute x5, waiting for transfers between devices, swap(): return lax.ppermute(value, 'seq', [(0, 1), (1, 0)])  9.82 us
    all_to_all x1, starting transfers between devices, on_device_xla(): lax.all_to_all(total_score.reshape(n_expert, capacity), 'expert', split_a...  9.42 us
    all_to_all x1, waiting for transfers between devices, on_device_xla(): lax.all_to_all(total_score.reshape(n_expert, capacity), 'expert', split_a...  7.28 us
    all_to_all x1, starting transfers between devices, on_device_xla(): lax.all_to_all(total.reshape(n_expert, capacity, half), 'expert', split_a...  3.85 us
    select_n x3, other arithmetic, ordered(): low = jnp.where(seq_at == 0, mine, theirs)  3.14 us
  transfers between devices with their start and end apart: 7, of which 6 were waited for; matrix products, arithmetic and copies ran while one was open for 1% of the time, Pallas kernels for 0%

commit v1 on v0

--- a/solution.py
+++ b/solution.py
@@ -1,6 +1,10 @@
+import functools
+
 import jax
 import jax.numpy as jnp
 from jax import lax
+from jax.experimental import pallas as pl
+from jax.experimental.pallas import tpu as pltpu
 from jax.sharding import PartitionSpec as P
 
 BF = jnp.bfloat16
@@ -96,6 +100,441 @@
     return in_grad, weight_grad.astype(BF)
 
 
+MESH = pl.DeviceIdType.MESH
+PARTS = 4
+
+
+def lanes(shape, axis):
+    return lax.broadcasted_iota(jnp.int32, shape, axis).astype(F32)
+
+
+def fdiv(value, by):
+    return jnp.floor((value + 0.5) * (1.0 / by))
+
+
+def ones(mask):
+    return jnp.where(mask, 1.0, 0.0).astype(BF)
+
+
+def step_kernel(
+    n, cap, og, ids_ref, wt_ref, gp_ref, up_ref, wg_hbm, wu_hbm, wd_hbm,
+    out_ref, wgrad_ref,
+    wg, wu, wd, tok, snd, rxo, rxp, xo, xp, hid, gd, ud, pout, pin, ybuf, rx2, z,
+    vbuf, whi, wlo, scs, sci, sco, scr, osend,
+    s_tok, r_tok, l_tok, l_w, s_d, r_d, s_f, r_f, s_p, r_p, s_s, r_s, s_b, r_b, s_c, r_c,
+    s_o, r_o, l_o,
+):
+    me = lax.axis_index("expert")
+    s = lax.axis_index("seq")
+    o = 1 - s
+    own, width = og.shape
+    half = width // 2
+    slots = n * cap
+    blk = PARTS * cap
+    grp = PARTS * blk
+    rows = PARTS * cap
+    qw = half // PARTS
+    quads = n // PARTS
+    zat = me // PARTS
+
+    barrier = pltpu.get_barrier_semaphore()
+    pl.semaphore_signal(barrier, inc=1, device_id=(me, o), device_id_type=MESH)
+
+    def greet(i, c):
+        pl.semaphore_signal(
+            barrier, inc=1, device_id=(lax.rem(me + i, n), s), device_id_type=MESH
+        )
+        return c
+
+    lax.fori_loop(1, n, greet, 0)
+
+    base = pl.multiple_of(s * half, 128)
+    obase = pl.multiple_of(o * half, 128)
+    mine = pl.multiple_of(s * own, 16)
+    theirs = pl.multiple_of(o * own, 16)
+
+    local_tok = pltpu.make_async_copy(
+        og.at[:, pl.ds(base, half)], tok.at[pl.ds(mine, own), :], l_tok
+    )
+    local_tok.start()
+    pl.semaphore_wait(barrier, n)
+
+    def remote(src, dst, ss, rs, dev):
+        return pltpu.make_async_remote_copy(
+            src_ref=src, dst_ref=dst, send_sem=ss, recv_sem=rs, device_id=dev, device_id_type=MESH
+        )
+
+    tok_copy = remote(
+        og.at[:, pl.ds(obase, half)], tok.at[pl.ds(mine, own), :], s_tok, r_tok, (me, o)
+    )
+    tok_copy.start()
+    loads = [
+        pltpu.make_async_copy(wd_hbm, wd, l_w.at[0]),
+        pltpu.make_async_copy(wg_hbm, wg, l_w.at[1]),
+        pltpu.make_async_copy(wu_hbm, wu, l_w.at[2]),
+    ]
+
+    tokens = 2 * own
+    ids = ids_ref[...]
+    wts = wt_ref[...]
+    e_lane = lax.broadcasted_iota(jnp.int32, (tokens, n), 1)
+    hit = jnp.zeros((tokens, n), F32)
+    wte = jnp.zeros((tokens, n), F32)
+    for k in range(ids_ref.shape[1]):
+        same = ids[:, k : k + 1] == e_lane
+        hit = jnp.where(same, 1.0, hit)
+        wte = jnp.where(same, wts[:, k : k + 1], wte)
+    tri = ones(lanes((tokens, tokens), 1) < lanes((tokens, tokens), 0))
+    pos = dot(tri, hit.astype(BF), NN)
+    v = jnp.where((hit > 0.5) & (pos < cap - 0.5), pos, 255.0)
+    vbuf[...] = v
+    vb = v.astype(BF)
+    c = lanes((tokens, slots), 1)
+    place = c - cap * fdiv(c, cap)
+    ec = lanes((n, slots), 1)
+    expand = ones(fdiv(ec, cap) == lanes((n, slots), 0))
+    taken = dot(vb, expand, NN) == place
+    hi = wte.astype(BF)
+    lo = (wte - hi.astype(F32)).astype(BF)
+    whi[...] = jnp.where(taken, dot(hi, expand, NN), 0.0).astype(BF)
+    wlo[...] = jnp.where(taken, dot(lo, expand, NN), 0.0).astype(BF)
+    r0 = lanes((grp, grp), 0)
+    a0 = fdiv(r0, blk)
+    b0 = fdiv(r0 - a0 * blk, cap)
+    p0 = r0 - a0 * blk - b0 * cap
+    perm = ones(lanes((grp, grp), 1) == b0 * blk + a0 * cap + p0)
+
+    local_tok.wait()
+    tok_copy.wait_recv()
+
+    def d_copy(dest):
+        at = pl.multiple_of(dest * blk, 16)
+        to = pl.multiple_of(me * blk, 16)
+        return remote(
+            snd.at[pl.ds(at, blk), :], rxo.at[pl.ds(to, blk), :], s_d.at[dest], r_d.at[me], (dest, s)
+        )
+
+    def d_wait(src):
+        at = pl.multiple_of(src * blk, 16)
+        return remote(
+            snd.at[pl.ds(at, blk), :], rxo.at[pl.ds(at, blk), :], s_d.at[src], r_d.at[src], (src, s)
+        )
+
+    def f_copy(src):
+        at = pl.multiple_of(src * blk, 16)
+        return remote(
+            rxo.at[pl.ds(at, blk), :], rxp.at[pl.ds(at, blk), :], s_f.at[src], r_f.at[src], (me, o)
+        )
+
+    def own_copy():
+        at = pl.multiple_of(me * blk, 16)
+        return remote(
+            snd.at[pl.ds(at, blk), :], rxp.at[pl.ds(at, blk), :], s_f.at[me], r_f.at[me], (me, o)
+        )
+
+    def dispatch(i, carry):
+        quad = lax.rem(zat + 1 + i, quads)
+        rr = lanes((rows, n), 0)
+        pick = ones(fdiv(rr, cap) + (quad * PARTS).astype(F32) == lanes((rows, n), 1))
+        vt = dot(pick, vb, NT)
+        rt = lanes((rows, tokens), 0)
+        sel = ones(vt == rt - cap * fdiv(rt, cap))
+        stacked = jnp.concatenate(
+            [dot(sel, tok[:, q * qw : (q + 1) * qw], NN).astype(BF) for q in range(PARTS)], axis=0
+        )
+        snd[pl.ds(pl.multiple_of(quad * grp, 16), grp), :] = dot(perm, stacked, NN).astype(BF)
+        for j in range(PARTS):
+            dest = quad * PARTS + j
+
+            @pl.when(dest != me)
+            def _():
+                d_copy(dest).start()
+
+            @pl.when(dest == me)
+            def _():
+                at = pl.multiple_of(me * blk, 16)
+                rxo[pl.ds(at, blk), :] = snd[pl.ds(at, blk), :]
+                own_copy().start()
+
+        return carry
+
+    lax.fori_loop(0, quads, dispatch, 0)
+    for load in loads:
+        load.start()
+
+    def unpack(src, dst, quad):
+        got = dot(perm, src[pl.ds(pl.multiple_of(quad * grp, 16), grp), :], NN).astype(BF)
+        for q in range(PARTS):
+            dst[pl.ds(pl.multiple_of(quad * rows, 16), rows), q * qw : (q + 1) * qw] = got[
+                q * rows : (q + 1) * rows
+            ]
+
+    def collect(i, carry):
+        quad = lax.rem(zat + 2 * quads - 1 - i, quads)
+        for j in range(PARTS):
+            src = quad * PARTS + j
+
+            @pl.when(src != me)
+            def _():
+                d_wait(src).wait_recv()
+                f_copy(src).start()
+
+        unpack(rxo, xo, quad)
+        for j in range(PARTS):
+            f_copy(quad * PARTS + j).wait_recv()
+        unpack(rxp, xp, quad)
+        return carry
+
+    lax.fori_loop(0, quads, collect, 0)
+
+    hid[...] = jnp.zeros_like(hid)
+    loads[0].wait()
+    kw = 512
+
+    def hidden(i, carry):
+        at = pl.multiple_of(i * kw, 128)
+        hid[...] += dot(
+            xo[:, pl.ds(at, kw)], wd[:, pl.ds(pl.multiple_of(base + i * kw, 128), kw)], NT
+        ) + dot(xp[:, pl.ds(at, kw)], wd[:, pl.ds(pl.multiple_of(obase + i * kw, 128), kw)], NT)
+        return carry
+
+    lax.fori_loop(0, half // kw, hidden, 0)
+    active, slope = silu_parts(gp_ref[...].astype(F32))
+    up = up_ref[...].astype(F32)
+    grad = hid[...]
+    ud_v = grad * active
+    gd[...] = (grad * up * slope).astype(BF)
+    ud[...] = ud_v.astype(BF)
+    score = jnp.sum(ud_v * up, axis=1, keepdims=True)
+    scs[...] = jnp.broadcast_to(score, (slots, 128)).astype(BF)
+    sc_copy = remote(scs, sci, s_s, r_s, (me, o))
+    sc_copy.start()
+    loads[1].wait()
+    loads[2].wait()
+
+    def part(q, start):
+        at = pl.ds(pl.multiple_of(start + q * qw, 128), qw)
+        return (dot(gd[...], wg[at, :], NT) + dot(ud[...], wu[at, :], NT)).astype(BF)
+
+    def p_copy(q):
+        return remote(pout.at[q], pin.at[q], s_p.at[q], r_p.at[q], (me, o))
+
+    def give(q, carry):
+        pout[q] = part(q, obase)
+        p_copy(q).start()
+        return carry
+
+    lax.fori_loop(0, PARTS, give, 0)
+
+    def keep(q, carry):
+        value = part(q, base).astype(F32)
+        p_copy(q).wait_recv()
+        ybuf[q] = (value + pin[q].astype(F32)).astype(BF)
+        return carry
+
+    lax.fori_loop(0, PARTS, keep, 0)
+
+    sc_copy.wait_recv()
+    total = (scs[...].astype(F32) + sci[...].astype(F32)).astype(BF)
+    sr = lanes((n * 16, slots), 0)
+    se = fdiv(sr, 16)
+    sp = sr - 16 * se
+    spread = ones((lanes((n * 16, slots), 1) == se * cap + sp) & (sp < cap - 0.5))
+    sco[...] = dot(spread, total, NN).astype(BF)
+
+    def wait_d(i, carry):
+        d_copy(lax.rem(me + i, n)).wait_send()
+        f_copy(lax.rem(me + i, n)).wait_send()
+        return carry
+
+    lax.fori_loop(1, n, wait_d, 0)
+    own_copy().wait_send()
+
+    def b_copy(dest):
+        at = pl.multiple_of(dest * blk, 16)
+        to = pl.multiple_of(me * blk, 16)
+        return remote(
+            snd.at[pl.ds(at, blk), :], rx2.at[pl.ds(to, blk), :], s_b.at[dest], r_b.at[me], (dest, s)
+        )
+
+    def b_wait(src):
+        at = pl.multiple_of(src * blk, 16)
+        return remote(
+            snd.at[pl.ds(at, blk), :], rx2.at[pl.ds(at, blk), :], s_b.at[src], r_b.at[src], (src, s)
+        )
+
+    def c_copy(dest):
+        at = pl.multiple_of(dest * 16, 16)
+        to = pl.multiple_of(me * 16, 16)
+        return remote(
+            sco.at[pl.ds(at, 16), :], scr.at[pl.ds(to, 16), :], s_c.at[dest], r_c.at[me], (dest, s)
+        )
+
+    def c_wait(src):
+        at = pl.multiple_of(src * 16, 16)
+        return remote(
+            sco.at[pl.ds(at, 16), :], scr.at[pl.ds(at, 16), :], s_c.at[src], r_c.at[src], (src, s)
+        )
+
+    def combine_send(i, carry):
+        quad = lax.rem(zat + 1 + i, quads)
+        at = pl.ds(pl.multiple_of(quad * rows, 16), rows)
+        stacked = jnp.concatenate([ybuf[q, at, :] for q in range(PARTS)], axis=0)
+        snd[pl.ds(pl.multiple_of(quad * grp, 16), grp), :] = dot(perm, stacked, NN).astype(BF)
+        for j in range(PARTS):
+            dest = quad * PARTS + j
+
+            @pl.when(dest != me)
+            def _():
+                c_copy(dest).start()
+                b_copy(dest).start()
+
+            @pl.when(dest == me)
+            def _():
+                here = pl.ds(pl.multiple_of(me * blk, 16), blk)
+                rx2[here, :] = snd[here, :]
+                there = pl.ds(pl.multiple_of(me * 16, 16), 16)
+                scr[there, :] = sco[there, :]
+
+        return carry
+
+    lax.fori_loop(0, quads, combine_send, 0)
+
+    def collect2(i, carry):
+        quad = lax.rem(zat + 2 * quads - 1 - i, quads)
+        for j in range(PARTS):
+            src = quad * PARTS + j
+
+            @pl.when(src != me)
+            def _():
+                b_wait(src).wait_recv()
+                c_wait(src).wait_recv()
+
+        unpack(rx2, z, quad)
+        return carry
+
+    lax.fori_loop(0, quads, collect2, 0)
+
+    def rows_of(start, q):
+        zq = z[:, q * qw : (q + 1) * qw]
+        at = pl.ds(start, own)
+        return (dot(whi[at, :], zq, NN) + dot(wlo[at, :], zq, NN)).astype(BF)
+
+    def o_copy(q):
+        return remote(
+            osend.at[q],
+            out_ref.at[:, pl.ds(pl.multiple_of(base + q * qw, 128), qw)],
+            s_o.at[q], r_o.at[q], (me, o),
+        )
+
+    def o_wait(q):
+        return remote(
+            osend.at[q],
+            out_ref.at[:, pl.ds(pl.multiple_of(obase + q * qw, 128), qw)],
+            s_o.at[q], r_o.at[q], (me, o),
+        )
+
+    def o_local(q):
+        return pltpu.make_async_copy(
+            osend.at[PARTS + q],
+            out_ref.at[:, pl.ds(pl.multiple_of(base + q * qw, 128), qw)],
+            l_o.at[q],
+        )
+
+    for q in range(PARTS):
+        osend[q] = rows_of(theirs, q)
+        o_copy(q).start()
+    for q in range(PARTS):
+        osend[PARTS + q] = rows_of(mine, q)
+        o_local(q).start()
+
+    vo = vbuf[pl.ds(mine, own), :].astype(BF)
+    wide = n * 16
+    wc = lanes((own, wide), 1)
+    we = fdiv(wc, 16)
+    spot = dot(vo, ones(fdiv(lanes((n, wide), 1), 16) == lanes((n, wide), 0)), NN) == wc - 16 * we
+    ido = ids_ref[pl.ds(mine, own), :].astype(F32)
+    acc = jnp.zeros((own, 128), F32)
+    for k in range(ids_ref.shape[1]):
+        sel = ones(spot & (we == ido[:, k : k + 1]))
+        acc = jnp.where(lanes((own, 128), 1) == k, dot(sel, scr[...], NN), acc)
+    wgrad_ref[...] = acc[:, : wgrad_ref.shape[1]].astype(BF)
+
+    tok_copy.wait_send()
+    sc_copy.wait_send()
+
+    def drain(i, carry):
+        dest = lax.rem(me + i, n)
+        b_copy(dest).wait_send()
+        c_copy(dest).wait_send()
+        return carry
+
+    lax.fori_loop(1, n, drain, 0)
+    for q in range(PARTS):
+        p_copy(q).wait_send()
+        o_copy(q).wait_send()
+        o_local(q).wait()
+        o_wait(q).wait_recv()
+
+
+def scratch(n, cap, own, width, hidden):
+    half = width // 2
+    slots = n * cap
+    big = PARTS * slots
+    qw = half // PARTS
+    vm, dma = pltpu.VMEM, pltpu.SemaphoreType.DMA
+    return [
+        vm((width, hidden), BF), vm((width, hidden), BF), vm((hidden, width), BF),
+        vm((2 * own, half), BF), vm((big, qw), BF), vm((big, qw), BF), vm((big, qw), BF),
+        vm((slots, half), BF), vm((slots, half), BF), vm((slots, hidden), F32),
+        vm((slots, hidden), BF), vm((slots, hidden), BF),
+        vm((PARTS, slots, qw), BF), vm((PARTS, slots, qw), BF), vm((PARTS, slots, qw), BF),
+        vm((big, qw), BF), vm((slots, half), BF),
+        vm((2 * own, n), F32), vm((2 * own, slots), BF), vm((2 * own, slots), BF),
+        vm((slots, 128), BF), vm((slots, 128), BF), vm((n * 16, 128), BF), vm((n * 16, 128), BF),
+        vm((2 * PARTS, own, qw), BF),
+        dma, dma, dma, dma((3,)),
+        dma((n,)), dma((n,)), dma((n,)), dma((n,)), dma((PARTS,)), dma((PARTS,)), dma, dma,
+        dma((n,)), dma((n,)), dma((n,)), dma((n,)), dma((PARTS,)), dma((PARTS,)), dma((PARTS,)),
+    ]
+
+
+def kernel_fits(n, cap, own, width, hidden):
+    half = width // 2
+    slots = n * cap
+    size = 2 * (3 * width * hidden + 10 * slots * half + 4 * own * half)
+    aligned = (PARTS * cap) % 16 == 0 and half % (PARTS * 128) == 0 and half % 512 == 0
+    return n % PARTS == 0 and cap <= 16 and aligned and own % 16 == 0 and size < 48 * 2**20
+
+
+def on_device(out_grad, route_ids, route_weights, gate_pre, up_pre, w_gate, w_up, w_down):
+    n = lax.axis_size("expert")
+    own, width = out_grad.shape
+    slots, hidden = gate_pre.shape[1:]
+    cap = slots // n
+    args = (out_grad, route_ids, route_weights, gate_pre, up_pre, w_gate, w_up, w_down)
+    if not kernel_fits(n, cap, own, width, hidden):
+        return on_device_xla(*args)
+    anywhere = pl.BlockSpec(memory_space=pl.ANY)
+    vmem = pl.BlockSpec(memory_space=pltpu.VMEM)
+    return pl.pallas_call(
+        functools.partial(step_kernel, n, cap),
+        out_shape=(
+            jax.ShapeDtypeStruct((own, width), BF),
+            jax.ShapeDtypeStruct((own, route_ids.shape[1]), BF),
+        ),
+        in_specs=[anywhere, vmem, vmem, vmem, vmem, anywhere, anywhere, anywhere],
+        out_specs=(anywhere, vmem),
+        scratch_shapes=scratch(n, cap, own, width, hidden),
+        compiler_params=pltpu.CompilerParams(
+            collective_id=0, has_side_effects=True, vmem_limit_bytes=63 * 2**20
+        ),
+        name="expert_step",
+    )(
+        out_grad, route_ids, route_weights, gate_pre[0], up_pre[0], w_gate[0], w_up[0], w_down[0]
+    )
+
+
 def solution(mesh):
     in_specs = (
         P(("expert", "seq"), None),
@@ -109,5 +548,5 @@
     )
     out_specs = (P(("expert", "seq"), None), P(("expert", "seq"), None))
     return jax.shard_map(
-        on_device_xla, mesh=mesh, in_specs=in_specs, out_specs=out_specs, check_vma=False
+        on_device, mesh=mesh, in_specs=in_specs, out_specs=out_specs, check_vma=False
     )

time: 151 us -> 103 us (0.68)
  the two profiles are of different devices: /device:TPU:0 before, /device:TPU:31 now
where the time goes in v1:
time: 103 us; the launch traced here: 102 us
  Pallas kernels  94.5 us (92%)
  local copies, waits for them, and re-layouts  7.21 us (7%)
    pallas_call x1, Pallas kernels, on_device(): pl.pallas_call(functools.partial(step_kernel, n, cap), out_shape=(jax.Sha...  94.5 us
    unnamed x3, local copies, waits for them, and re-layouts  5.81 us

profile of v1, /device:TPU:31, one launch (start us, length us, event | category | flops | bytes accessed | tf_op | source)
XLA Modules:
  0.0 102.4 jit_solution(7986765828140439029)
XLA Ops:
  0.6 1.5 %copy.10.ids_ref = s32[256,8]{1,0:T(8,128)} copy(s32[256,8]{0,1:T(8,128)} %param.9) | data formatting | bytes 16384 | tf_op args[1]
  2.1 1.5 %copy.11.wt_ref = f32[256,8]{1,0:T(8,128)} copy(f32[256,8]{0,1:T(8,128)} %param.10) | data formatting | bytes 16384 | tf_op args[2]
  3.6 94.5 %expert_step.1 = (bf16[128,7168]{1,0:T(8,128)(2,1)}, bf16[128,8]{1,0:T(8,128)(2,1)}) custom-call(bf16[128,7168]{1,0:T(8,128)(2,1)} %og.1, s32[256,8]{1,0:T(8,128)} %copy.10.ids_ref, f32[256,8]{1,0:T(8,128)} %copy.11.wt_ref, bf16[192,512]{1,0:T(8,128)(2,1)} %bitcast.8, bf16[192,512]{1,0:T(8,128)(2,1)} %bitcast.9, bf16[7168,512]{1,0:T(8,128)(2,1)} %bitcast.5, ...), custom_call_target="tpu_custom_call" | custom-call | tf_op jit(solution)/shard_map/expert_step/pallas_call | solution.py:520
  98.1 1.4 %copy.12 = bf16[128,8]{0,1:T(8,128)(2,1)} copy(bf16[128,8]{1,0:T(8,128)(2,1)} %get-tuple-element.3) | data formatting | bytes 4096 | tf_op jit(solution)/shard_map/expert_step/pallas_call | solution.py:520
  99.6 2.8 %copy.14 = bf16[128,7168]{1,0:T(8,128)(2,1)} copy(bf16[128,7168]{1,0:T(8,128)(2,1)} %get-tuple-element.6) | data formatting | bytes 3670016
